TPU v7x, 32 devices: a whole 2x2x4 slice. The times are simulated.
32 devices in a mesh: chan: 4 (over y, core), blk: 8 (over z, x).
Axes of the slice: x: 2, y: 2, z: 4, core: 2. Of those that a mesh axis runs over, the one named last changes fastest.
Arguments:
- comp_alms: float32 [3, 4, 8, 4096], P(None, None, 'blk', 'chan'), may hold values from -6 to 6
- legendre: bfloat16 [2, 8, 4096, 32], P(None, 'blk'), may hold values from -0.09375 to 0.09375
- inv_noise: float32 [4, 2, 32, 8192], P('chan', None, 'blk'), may hold values from 0.5 to 5
- beam_window: float32 [4, 4096], replicated, may hold values from 0.1 to 1
- mixing: float32 [4, 3], replicated, may hold values from 0.2 to 1.5
- channel_of: int32 [4], replicated, may hold values from 0 to 3, each once
- m_orders: int32 [8], replicated, may hold values from 0 to 4095, as said below
- cycle_of: int32 [32], replicated, may hold values from 0 to 31, each once
- cycle_pixels: int32 [32], replicated, may hold values from 4 to 8192, as said below
Outputs:
- normal_product: float32 [3, 4, 8, 4096], P(None, None, 'blk', 'chan')
Inputs may be any that keep to these rules, and one draw needn't show every extreme that they name: `m_orders`: the orders are distinct. `cycle_pixels`: each entry is 4 * min(h, 2048, 8192 - h) for some cycle number h of 1 to 8191; at least one entry equals 8192.
All inputs are finite; a program needn't handle non-finite values.
Results may differ from a plain program's by a relative error of at most 0.0022.
Values may be sent and summed in bfloat16 or wider, within the bound.
A program may use at most 128 MiB of HBM per device.

v0:
```python
import math
import jax
import jax.numpy as jnp
from jax import lax
from jax.sharding import PartitionSpec as P


def phase_rows(orders, pix_count, cycle_width):
    columns = jnp.arange(cycle_width, dtype=jnp.int32)
    phase_steps = orders[:, None] * (2 * columns[None, :] + 1) % (2 * pix_count)
    angles = phase_steps.astype(jnp.float32) * (
        jnp.float32(math.pi) / pix_count.astype(jnp.float32)
    )
    return jnp.concatenate([jnp.cos(angles), jnp.sin(angles)], axis=0).astype(jnp.bfloat16)


def combine_forward(plus_sum, minus_sum):
    return jnp.stack(
        [
            plus_sum[:, 0] - minus_sum[:, 3],
            plus_sum[:, 1] + minus_sum[:, 2],
            plus_sum[:, 2] + minus_sum[:, 1],
            plus_sum[:, 3] - minus_sum[:, 0],
        ],
        axis=1,
    )


def twist_grads(cycle_grads):
    return jnp.stack(
        [-cycle_grads[:, 3], cycle_grads[:, 2], cycle_grads[:, 1], -cycle_grads[:, 0]], axis=1
    )


def cycle_work(coeffs, weights, orders, pix_count):
    slots = coeffs.shape[0]
    cycle_width = weights.shape[-1]
    phases = phase_rows(orders, pix_count, cycle_width)
    half_rows = phases.shape[0] // 2
    real_part = coeffs[:, 0::2]
    imag_part = coeffs[:, 1::2]
    stacked = jnp.concatenate([real_part, -imag_part], axis=2).reshape(2 * slots, 2 * half_rows)
    maps = jnp.dot(stacked, phases, preferred_element_type=jnp.float32)
    live_mask = jnp.arange(cycle_width, dtype=jnp.int32) < pix_count
    scaled = jnp.where(live_mask[None, None, :], weights, 0.0) / pix_count.astype(jnp.float32)
    weighted = (scaled.reshape(maps.shape) * maps).astype(jnp.bfloat16)
    returned = lax.dot_general(
        weighted, phases, (((1,), (1,)), ((), ())), preferred_element_type=jnp.float32
    )
    grad_real = returned[:, :half_rows].reshape(slots, 2, half_rows)
    grad_imag = (-returned[:, half_rows:]).reshape(slots, 2, half_rows)
    return (
        jnp.stack([grad_real, grad_imag], axis=2).reshape(slots, 4, half_rows).astype(jnp.bfloat16)
    )


def mix_components(mix_rows, components):
    accum = mix_rows[:, 0, None, None, None] * components[0][None]
    for comp_index in range(1, components.shape[0]):
        accum = accum + mix_rows[:, comp_index, None, None, None] * components[comp_index][None]
    return accum


def body(
    comp_alms,
    legendre,
    inv_noise,
    beam_window,
    mixing,
    channel_of,
    m_orders,
    cycle_of,
    cycle_pixels,
):
    chan_index = lax.axis_index("chan")
    blk_index = lax.axis_index("blk")
    order_dev = comp_alms.shape[2]
    shard_len = comp_alms.shape[3]
    length = legendre.shape[2]
    cycle_total = legendre.shape[3]
    chan_dev = inv_noise.shape[0]
    cycle_dev = inv_noise.shape[2]
    block_len = min(512, length)
    blocks = length // block_len
    own_orders = lax.dynamic_slice_in_dim(m_orders, blk_index * order_dev, order_dev)
    keep_mask = (jnp.arange(length, dtype=jnp.int32)[None, :] >= own_orders[:, None]).astype(
        jnp.float32
    )
    picked = lax.dynamic_slice_in_dim(channel_of, chan_index * chan_dev, chan_dev)
    mix_rows = jnp.take(mixing, picked, axis=0)
    beam_rows = jnp.take(beam_window, picked, axis=0)
    mix_all = jnp.take(mixing, channel_of, axis=0)
    beam_piece = jnp.take(
        lax.dynamic_slice_in_dim(beam_window, chan_index * shard_len, shard_len, 1),
        channel_of,
        axis=0,
    )
    gathered = lax.all_gather(comp_alms, "chan", axis=3, tiled=True)
    mixed_alm = mix_components(mix_rows, gathered)
    chan_alm = (mixed_alm * beam_rows[:, None, None, :] * keep_mask[None, None]).astype(
        jnp.bfloat16
    )
    order = 0
    row_block = chan_alm[:, :, order, :].reshape(chan_dev * 4, length)
    first_block = own_orders[order] // block_len

    def add_block(index, running, row_block=row_block, order=order):
        plus_sum, minus_sum = running
        offset = index * block_len
        segment = lax.dynamic_slice_in_dim(row_block, offset, block_len, 1)
        tables = lax.dynamic_slice(legendre, (0, order, offset, 0), (2, 1, block_len, cycle_total))
        plus_sum = plus_sum + jnp.dot(segment, tables[0, 0], preferred_element_type=jnp.float32)
        minus_sum = minus_sum + jnp.dot(segment, tables[1, 0], preferred_element_type=jnp.float32)
        return (plus_sum, minus_sum)

    zeros_cycle = jnp.zeros((chan_dev * 4, cycle_total), jnp.float32)
    plus_sum, minus_sum = lax.fori_loop(first_block, blocks, add_block, (zeros_cycle, zeros_cycle))
    coeff_list = [
        combine_forward(
            plus_sum.reshape(chan_dev, 4, cycle_total), minus_sum.reshape(chan_dev, 4, cycle_total)
        )
    ]
    cycle_coeffs = jnp.stack(coeff_list, axis=2).astype(jnp.bfloat16)
    slot_coeffs = jnp.take(cycle_coeffs, cycle_of, axis=3)
    by_cycle = lax.all_to_all(slot_coeffs, "blk", split_axis=3, concat_axis=2, tiled=True)
    first_slot = blk_index * cycle_dev

    def per_cycle(index, collected):
        coeffs = lax.dynamic_index_in_dim(by_cycle, index, 3, keepdims=False)
        weights = lax.dynamic_index_in_dim(inv_noise, index, 2, keepdims=False)
        pix_count = cycle_pixels[cycle_of[first_slot + index]]
        result = cycle_work(coeffs, weights, m_orders, pix_count)
        return lax.dynamic_update_index_in_dim(collected, result, index, 3)

    slot_grads = lax.fori_loop(0, cycle_dev, per_cycle, jnp.zeros(by_cycle.shape, jnp.bfloat16))
    returned = lax.all_to_all(slot_grads, "blk", split_axis=2, concat_axis=3, tiled=True)
    inverse = (
        jnp.zeros((cycle_total,), jnp.int32)
        .at[cycle_of]
        .set(jnp.arange(cycle_total, dtype=jnp.int32))
    )
    cycle_grads = jnp.take(returned, inverse, axis=3)
    order = 0
    order_grads = cycle_grads[:, :, order, :]
    twisted = twist_grads(order_grads).reshape(chan_dev * 4, cycle_total)
    straight = order_grads.reshape(chan_dev * 4, cycle_total)
    first_block = own_orders[order] // block_len

    def add_degrees(index, accum, straight=straight, twisted=twisted, order=order):
        offset = index * block_len
        tables = lax.dynamic_slice(legendre, (0, order, offset, 0), (2, 1, block_len, cycle_total))
        segment = lax.dot_general(
            straight, tables[0, 0], (((1,), (1,)), ((), ())), preferred_element_type=jnp.float32
        )
        segment = segment + lax.dot_general(
            twisted, tables[1, 0], (((1,), (1,)), ((), ())), preferred_element_type=jnp.float32
        )
        return lax.dynamic_update_slice_in_dim(accum, segment, offset, 1)

    accum = lax.fori_loop(
        first_block, blocks, add_degrees, jnp.zeros((chan_dev * 4, length), jnp.float32)
    )
    grad_list = [accum.reshape(chan_dev, 4, length)]
    alm_grads = jnp.stack(grad_list, axis=2) * keep_mask[None, None]
    received = lax.all_to_all(alm_grads, "chan", split_axis=3, concat_axis=0, tiled=True)
    beamed = received * beam_piece[:, None, None, :]
    return jnp.einsum("kc,kpml->cpml", mix_all, beamed, precision=lax.Precision.HIGHEST)


def solution(mesh):
    in_specs = (
        P(None, None, "blk", "chan"),
        P(None, "blk", None, None),
        P("chan", None, "blk", None),
        P(),
        P(),
        P(),
        P(),
        P(),
        P(),
    )
    out_specs = P(None, None, "blk", "chan")
    return jax.shard_map(body, mesh=mesh, in_specs=in_specs, out_specs=out_specs, check_vma=False)
```

profile of v0, /device:TPU:8, one launch (start us, length us, event | category | flops | bytes accessed | tf_op | source)
XLA Modules:
  0.0 151.8 jit_solution(12657113365354323406)
XLA Ops:
  0.0 1.2 dynamic_slice.48
  5.2 1.3 dynamic_slice.49
  11.4 5.6 %all_gather.3 = f32[3,4,1,4096]{3,1,2,0:T(4,128)S(1)} all-gather(f32[3,4,1,1024]{3,1,2,0:T(4,128)S(1)} %copy.31), channel_id=1, replica_groups=mesh['chan'=4,'blk'=8] {'chan'}, dimensions={3}, use_global_device_ids=true | all-gather | bytes 245760 | tf_op jit(solution)/shard_map/all_gather | solution.py:98
  17.6 1.9 %fusion.43 = bf16[4,4096]{1,0:T(4,128)(2,1)S(1)} fusion(f32[4096]{0:T(1024)S(1)} %fusion.44, f32[4096]{0:T(1024)S(1)} %bitcast.126, f32[3,4,1,4096]{3,1,2,0:T(4,128)S(1)} %all_gather.3, f32[]{:T(128)} %bitcast.19, f32[]{:T(128)} %bitcast.18, f32[]{:T(128)} %bitcast.17), kind=kLoop, calls=%fused_computation.70 | loop fusion | flops 131072 | bytes 262156 | tf_op jit(solution)/shard_map/reshape;squeeze | solution.py:104
  19.6 8.9 %while.37 = (s32[]{:T(128)}, f32[4,32]{1,0:T(4,128)S(1)}, f32[4,32]{1,0:T(4,128)S(1)}, bf16[4,4096]{1,0:T(4,128)(2,1)S(1)}, bf16[2,1,4096,32]{2,3,1,0:T(8,128)(2...) while((s32[]{:T(128)}, f32[4,32]{1,0:T(4,128)S(1)}, f32[4,32]{1,0:T(4,128)S(1)}, ...), condition=%wide.region_1.2_spmd, body=%wide.region_0.1_spmd.sunk | while | flops 262407 | bytes 81567 | solution.py:117
  30.0 5.3 %all-to-all-start = ((bf16[1,4,1,32]{1,2,0,3:T(2,128)(2,1)}), bf16[1,4,1,32]{1,2,0,3:T(2,128)(2,1)S(1)}, u32[]{:S(2)}, u32[]{:S(2)}) async-start(bf16[1,4,1,32]{1,2,0,3:T(2,128)(2,1)} %copy.34), calls=%async_computation | async-start | bytes 32768 | tf_op jit(solution)/shard_map/all_to_all | solution.py:125
  38.1 2.3 %all-to-all-done = bf16[1,4,1,32]{1,2,0,3:T(2,128)(2,1)S(1)} async-done(((bf16[1,4,1,32]{1,2,0,3:T(2,128)(2,1)}), bf16[1,4,1,32]{1,2,0,3:T(2,128)(2,1)S(1)}, u32[]{:S(2)}, u32[]{:S(2)}) %all-to-all-start) | async-done | bytes 288 | tf_op jit(solution)/shard_map/all_to_all | solution.py:125
  40.5 50.0 %while.38 = (s32[]{:T(128)}, bf16[1,4,8,4]{2,1,3,0:T(4,128)(2,1)S(1)}, s32[]{:T(128)}, s32[32]{0:T(128)}, s32[32]{0:T(128)}, /*index=5*/f32[1,2,4,8192]{3,2,1,0:...) while((s32[]{:T(128)}, ...), condition=%wide.region_3.5_spmd, body=%wide.region_2.4_spmd.sunk | while | flops 2973951 | bytes 806209 | solution.py:135
  40.5 1.2 dynamic_slice.68
  43.7 1.2 dynamic_slice.69
  46.3 4.4 %cosine_convert_fusion.2 = (bf16[8,8192]{1,0:T(8,128)(2,1)S(1)}, bf16[8,8192]{1,0:T(8,128)(2,1)S(1)}) fusion(f32[]{:T(128)S(6)} %div.51, s32[]{:T(128)S(6)} %select_n.210, s32[8192]{0:T(1024)S(1)} %multiply_add_fusion.2, s32[8]{0:T(128)} %get-tuple-element.485, pred[]{:T(512)S(6)} %lt.154), kind=kLoop, calls=%fused_computation.23.clone.1 | loop fusion | flops 786432 | bytes 294953 | tf_op jit(solution)/shard_map/convert.5
  51.4 1.0 constant_dynamic-slice_fusion.4
  53.0 1.2 dynamic_slice.68
  56.2 1.2 dynamic_slice.69
  58.8 4.4 %cosine_convert_fusion.2 = (bf16[8,8192]{1,0:T(8,128)(2,1)S(1)}, bf16[8,8192]{1,0:T(8,128)(2,1)S(1)}) fusion(f32[]{:T(128)S(6)} %div.51, s32[]{:T(128)S(6)} %select_n.210, s32[8192]{0:T(1024)S(1)} %multiply_add_fusion.2, s32[8]{0:T(128)} %get-tuple-element.485, pred[]{:T(512)S(6)} %lt.154), kind=kLoop, calls=%fused_computation.23.clone.1 | loop fusion | flops 786432 | bytes 294953 | tf_op jit(solution)/shard_map/convert.5
  65.5 1.2 dynamic_slice.68
  68.7 1.2 dynamic_slice.69
  71.3 4.4 %cosine_convert_fusion.2 = (bf16[8,8192]{1,0:T(8,128)(2,1)S(1)}, bf16[8,8192]{1,0:T(8,128)(2,1)S(1)}) fusion(f32[]{:T(128)S(6)} %div.51, s32[]{:T(128)S(6)} %select_n.210, s32[8192]{0:T(1024)S(1)} %multiply_add_fusion.2, s32[8]{0:T(128)} %get-tuple-element.485, pred[]{:T(512)S(6)} %lt.154), kind=kLoop, calls=%fused_computation.23.clone.1 | loop fusion | flops 786432 | bytes 294953 | tf_op jit(solution)/shard_map/convert.5
  76.4 1.0 constant_dynamic-slice_fusion.4
  78.0 1.2 dynamic_slice.68
  81.2 1.2 dynamic_slice.69
  83.8 4.4 %cosine_convert_fusion.2 = (bf16[8,8192]{1,0:T(8,128)(2,1)S(1)}, bf16[8,8192]{1,0:T(8,128)(2,1)S(1)}) fusion(f32[]{:T(128)S(6)} %div.51, s32[]{:T(128)S(6)} %select_n.210, s32[8192]{0:T(1024)S(1)} %multiply_add_fusion.2, s32[8]{0:T(128)} %get-tuple-element.485, pred[]{:T(512)S(6)} %lt.154), kind=kLoop, calls=%fused_computation.23.clone.1 | loop fusion | flops 786432 | bytes 294953 | tf_op jit(solution)/shard_map/convert.5
  91.2 4.8 %all-to-all-start.1 = ((bf16[1,4,8,4]{1,3,0,2:T(4,128)(2,1)}), bf16[1,4,8,4]{1,3,0,2:T(4,128)(2,1)S(1)}, u32[]{:S(2)}, u32[]{:S(2)}) async-start(bf16[1,4,8,4]{1,3,0,2:T(4,128)(2,1)} %copy.38), calls=%async_computation.1 | async-start | bytes 16384 | tf_op jit(solution)/shard_map/all_to_all | solution.py:136
  96.6 4.5 %all-to-all-done.1 = bf16[1,4,8,4]{1,3,0,2:T(4,128)(2,1)S(1)} async-done(((bf16[1,4,8,4]{1,3,0,2:T(4,128)(2,1)}), bf16[1,4,8,4]{1,3,0,2:T(4,128)(2,1)S(1)}, u32[]{:S(2)}, u32[]{:S(2)}) %all-to-all-start.1) | async-done | bytes 288 | tf_op jit(solution)/shard_map/all_to_all | solution.py:136
  101.8 8.8 %while.39 = (s32[]{:T(128)}, f32[4,4096]{1,0:T(4,128)S(1)}, bf16[2,1,4096,32]{2,3,1,0:T(8,128)(2,1)}, bf16[4,32]{1,0:T(4,128)(2,1)S(1)}, bf16[4,32]{1,0:T(4,128)...) while((s32[]{:T(128)}, f32[4,4096]{1,0:T(4,128)S(1)}, ...), condition=%wide.region_6.8_spmd, body=%wide.region_5.7_spmd.sunk | while | flops 264199 | bytes 93091 | solution.py:160
  110.6 2.0 %copy.42 = f32[4,4096]{0,1:T(8,128)} copy(f32[4,4096]{1,0:T(4,128)S(1)} %get-tuple-element.203) | data formatting | bytes 131072 | tf_op jit(solution)/shard_map/while | solution.py:160
  112.6 2.2 %broadcast_multiply_fusion = f32[4,4096]{0,1:T(8,128)S(1)} fusion(f32[4,4096]{0,1:T(8,128)} %copy.42, f32[4096]{0:T(1024)S(1)} %fusion.44), kind=kLoop, calls=%fused_computation.58 | loop fusion | flops 16384 | bytes 147456 | tf_op jit(solution)/shard_map/mul | solution.py:164
  115.3 19.4 %reduce = f32[4096,4]{1,0:T(8,128)} reduce(f32[4096,1,1,4]{3,2,1,0:T(1,128)S(1)} %bitcast.121, f32[]{:T(128)} %broadcast.233), dimensions={1,2}, to_apply=%bitcast.83.reduce_sub_computation | reduce | bytes 131076
  134.7 3.9 %reshape.357 = f32[4,1,4096]{2,1,0:T(1,128)} reshape(f32[4096,4]{1,0:T(8,128)} %reduce) | data formatting | bytes 131072
  138.6 3.5 %all-to-all-start.2 = ((f32[4,1,4096]{2,1,0:T(1,128)}), f32[4,1,4096]{2,1,0:T(1,128)S(1)}, u32[]{:S(2)}, u32[]{:S(2)}) async-start(f32[4,1,4096]{2,1,0:T(1,128)} %reshape.357), calls=%async_computation.2 | async-start | bytes 131072 | tf_op jit(solution)/shard_map/all_to_all | solution.py:165
  142.7 3.3 %all-to-all-done.2 = f32[4,1,4096]{2,1,0:T(1,128)S(1)} async-done(((f32[4,1,4096]{2,1,0:T(1,128)}), f32[4,1,4096]{2,1,0:T(1,128)S(1)}, u32[]{:S(2)}, u32[]{:S(2)}) %all-to-all-start.2) | async-done | bytes 65568 | tf_op jit(solution)/shard_map/all_to_all | solution.py:165
  146.8 3.3 %reshape.358 = f32[4096,1,1,4]{3,2,1,0:T(1,128)S(1)} reshape(f32[4,4096]{1,0:T(4,128)S(1)} %reduce.1) | data formatting | bytes 131072
  (116 shorter events, 39.8 us)
Async XLA Ops:
  30.0 10.4 %all-to-all-start = ((bf16[1,4,1,32]{1,2,0,3:T(2,128)(2,1)}), bf16[1,4,1,32]{1,2,0,3:T(2,128)(2,1)S(1)}, u32[]{:S(2)}, u32[]{:S(2)}) async-start(bf16[1,4,1,32]{1,2,0,3:T(2,128)(2,1)} %copy.34), calls=%async_computation | async-start | bytes 32768 | tf_op jit(solution)/shard_map/all_to_all | solution.py:125
  91.2 9.8 %all-to-all-start.1 = ((bf16[1,4,8,4]{1,3,0,2:T(4,128)(2,1)}), bf16[1,4,8,4]{1,3,0,2:T(4,128)(2,1)S(1)}, u32[]{:S(2)}, u32[]{:S(2)}) async-start(bf16[1,4,8,4]{1,3,0,2:T(4,128)(2,1)} %copy.38), calls=%async_computation.1 | async-start | bytes 16384 | tf_op jit(solution)/shard_map/all_to_all | solution.py:136
  134.7 7.5 %copy-start = (f32[4,3]{1,0:T(4,128)S(1)}, f32[4,3]{1,0:T(4,128)}, u32[]{:S(2)}) copy-start(f32[4,3]{1,0:T(4,128)} %param.21) | copy-start | bytes 148
  138.6 7.4 %all-to-all-start.2 = ((f32[4,1,4096]{2,1,0:T(1,128)}), f32[4,1,4096]{2,1,0:T(1,128)S(1)}, u32[]{:S(2)}, u32[]{:S(2)}) async-start(f32[4,1,4096]{2,1,0:T(1,128)} %reshape.357), calls=%async_computation.2 | async-start | bytes 131072 | tf_op jit(solution)/shard_map/all_to_all | solution.py:165
where the time goes:
time: 154 us; the launch traced here: 152 us
  other arithmetic  49.9 us (32%)
  local copies, waits for them, and re-layouts  34.9 us (23%)
  matrix products  19.7 us (13%)
  starting transfers between devices  13.6 us (9%)
  loops' own time  13.5 us (9%)
  waiting for transfers between devices  10 us (6%)
  blocking collectives  5.6 us (4%)
  between operations  4.67 us (3%)
    unnamed x1, other arithmetic  19.4 us
    another operation x5, other arithmetic  17.5 us
    another operation x1, loops' own time, body(): lax.fori_loop(0, cycle_dev, per_cycle, jnp.zeros(by_cycle.shape, jnp.bflo...  13.4 us
    dynamic_slice x8, local copies, waits for them, and re-layouts, per_cycle(): pix_count = cycle_pixels[cycle_of[first_slot + index]]  9.93 us
    unnamed x7, local copies, waits for them, and re-layouts  8.55 us
    all_gather x1, blocking collectives, body(): gathered = lax.all_gather(comp_alms, 'chan', axis=3, tiled=True)  5.6 us
    all_to_all x1, starting transfers between devices, body(): lax.all_to_all(slot_coeffs, 'blk', split_axis=3, concat_axis=2, tiled=True)  5.32 us
    all_to_all x1, starting transfers between devices, body(): lax.all_to_all(slot_grads, 'blk', split_axis=2, concat_axis=3, tiled=True)  4.79 us
  transfers between devices with their start and end apart: 3, of which 3 were waited for; matrix products, arithmetic and copies ran while one was open for 3% of the time, Pallas kernels for 0%

commit v1 on v0

--- a/solution.py
+++ b/solution.py
@@ -3,6 +3,28 @@
 import jax.numpy as jnp
 from jax import lax
 from jax.sharding import PartitionSpec as P
+
+
+def cut_along(x, dim, size):
+    before, after = (x.shape[:dim], x.shape[dim + 1 :])
+    return jnp.moveaxis(x.reshape(*before, size, -1, *after), dim, 0)
+
+
+def laid_out(blocks, dim):
+    blocks = jnp.moveaxis(blocks, 0, dim)
+    dims = blocks.shape
+    return blocks.reshape(*dims[:dim], dims[dim] * dims[dim + 1], *dims[dim + 2 :])
+
+
+def pairwise_exchange(x, axis, split_dim, concat_dim):
+    count, index = (lax.axis_size(axis), lax.axis_index(axis))
+    parts = cut_along(x, split_dim, count)
+    outs = [parts[index]]
+    for turn in range(1, count):
+        sent = parts[index ^ turn]
+        outs.append(lax.ppermute(sent, axis, [(i, i ^ turn) for i in range(count)]))
+    parts = jnp.stack(outs)[index ^ jnp.arange(count)]
+    return laid_out(parts, concat_dim)
 
 
 def phase_rows(orders, pix_count, cycle_width):
@@ -162,7 +184,7 @@
     )
     grad_list = [accum.reshape(chan_dev, 4, length)]
     alm_grads = jnp.stack(grad_list, axis=2) * keep_mask[None, None]
-    received = lax.all_to_all(alm_grads, "chan", split_axis=3, concat_axis=0, tiled=True)
+    received = pairwise_exchange(alm_grads, "chan", 3, 0)
     beamed = received * beam_piece[:, None, None, :]
     return jnp.einsum("kc,kpml->cpml", mix_all, beamed, precision=lax.Precision.HIGHEST)
 

time: 154 us -> 109 us (0.71)
  the two profiles are of different devices: /device:TPU:8 before, /device:TPU:9 now
where the time goes in v1:
time: 109 us; the launch traced here: 107 us
  other arithmetic  21.7 us (20%)
  matrix products  19.7 us (18%)
  local copies, waits for them, and re-layouts  19 us (17%)
  starting transfers between devices  13.8 us (13%)
  loops' own time  13.5 us (12%)
  waiting for transfers between devices  8.34 us (8%)
  blocking collectives  6.11 us (6%)
  between operations  4.74 us (4%)
    another operation x5, other arithmetic  14.8 us
    another operation x1, loops' own time, body(): lax.fori_loop(0, cycle_dev, per_cycle, jnp.zeros(by_cycle.shape, jnp.bflo...  13.4 us
    all_gather x1, blocking collectives, body(): gathered = lax.all_gather(comp_alms, 'chan', axis=3, tiled=True)  6.11 us
    all_to_all x1, starting transfers between devices, body(): lax.all_to_all(slot_coeffs, 'blk', split_axis=3, concat_axis=2, tiled=True)  4.76 us
    dynamic_slice x8, local copies, waits for them, and re-layouts, per_cycle(): pix_count = cycle_pixels[cycle_of[first_slot + index]]  4.69 us
    ppermute x3, starting transfers between devices, pairwise_exchange(): outs.append(lax.ppermute(sent, axis, [(i, i ^ turn) for i in range(count)]))  4.52 us
    all_to_all x1, starting transfers between devices, body(): lax.all_to_all(slot_grads, 'blk', split_axis=2, concat_axis=3, tiled=True)  4.51 us
    dot_general x5, matrix products, add_block(): jnp.dot(segment, tables[1, 0], preferred_element_type=jnp.float32)  4.44 us
  transfers between devices with their start and end apart: 5, of which 4 were waited for; matrix products, arithmetic and copies ran while one was open for 2% of the time, Pallas kernels for 0%

profile of v1, /device:TPU:9, one launch (start us, length us, event | category | flops | bytes accessed | tf_op | source)
XLA Modules:
  0.0 106.8 jit_solution(16600595084187204178)
XLA Ops:
  8.0 6.1 %all_gather.3 = f32[3,4,1,4096]{3,1,2,0:T(4,128)S(1)} all-gather(f32[3,4,1,1024]{3,1,2,0:T(4,128)S(1)} %copy.36), channel_id=1, replica_groups=mesh['chan'=4,'blk'=8] {'chan'}, dimensions={3}, use_global_device_ids=true | all-gather | bytes 245760 | tf_op jit(solution)/shard_map/all_gather | solution.py:120
  14.8 1.9 %fusion.43 = bf16[4,4096]{1,0:T(4,128)(2,1)S(1)} fusion(f32[4096]{0:T(1024)S(1)} %fusion.44, f32[4096]{0:T(1024)S(1)} %bitcast.135, f32[3,4,1,4096]{3,1,2,0:T(4,128)S(1)} %all_gather.3, f32[]{:T(128)} %bitcast.19, f32[]{:T(128)} %bitcast.18, f32[]{:T(128)} %bitcast.17), kind=kLoop, calls=%fused_computation.72 | loop fusion | flops 131072 | bytes 262156 | tf_op jit(solution)/shard_map/reshape;squeeze | solution.py:126
  16.7 8.9 %while.37 = (s32[]{:T(128)}, f32[4,32]{1,0:T(4,128)S(1)}, f32[4,32]{1,0:T(4,128)S(1)}, bf16[4,4096]{1,0:T(4,128)(2,1)S(1)}, bf16[2,1,4096,32]{2,3,1,0:T(8,128)(2...) while((s32[]{:T(128)}, f32[4,32]{1,0:T(4,128)S(1)}, f32[4,32]{1,0:T(4,128)S(1)}, ...), condition=%wide.region_1.2_spmd, body=%wide.region_0.1_spmd.sunk | while | flops 262407 | bytes 81567 | solution.py:139
  16.7 0.9 convolution_add_fusion.6
  17.6 0.9 convolution_add_fusion.5
  18.5 0.9 convolution_add_fusion.6
  19.4 0.9 convolution_add_fusion.5
  20.3 0.9 convolution_add_fusion.6
  21.2 0.9 convolution_add_fusion.5
  22.1 0.9 convolution_add_fusion.6
  23.0 0.9 convolution_add_fusion.5
  23.8 0.9 convolution_add_fusion.6
  24.7 0.9 convolution_add_fusion.5
  27.2 4.8 %all-to-all-start = ((bf16[1,4,1,32]{1,2,0,3:T(2,128)(2,1)}), bf16[1,4,1,32]{1,2,0,3:T(2,128)(2,1)S(1)}, u32[]{:S(2)}, u32[]{:S(2)}) async-start(bf16[1,4,1,32]{1,2,0,3:T(2,128)(2,1)} %copy.39), calls=%async_computation | async-start | bytes 32768 | tf_op jit(solution)/shard_map/all_to_all | solution.py:147
  34.1 2.0 %all-to-all-done = bf16[1,4,1,32]{1,2,0,3:T(2,128)(2,1)S(1)} async-done(((bf16[1,4,1,32]{1,2,0,3:T(2,128)(2,1)}), bf16[1,4,1,32]{1,2,0,3:T(2,128)(2,1)S(1)}, u32[]{:S(2)}, u32[]{:S(2)}) %all-to-all-start) | async-done | bytes 288 | tf_op jit(solution)/shard_map/all_to_all | solution.py:147
  36.8 42.1 %while.38 = (s32[]{:T(128)}, bf16[1,4,8,4]{2,1,3,0:T(4,128)(2,1)S(1)}, s32[]{:T(128)}, s32[32]{0:T(128)S(1)}, s32[32]{0:T(128)S(1)}, /*index=5*/f32[1,2,4,8192]{...) while((s32[]{:T(128)}, ...), condition=%wide.region_3.5_spmd, body=%wide.region_2.4_spmd.sunk | while | flops 2973951 | bytes 806209 | solution.py:157
  41.2 3.7 %cosine_convert_fusion.2 = (bf16[8,8192]{1,0:T(8,128)(2,1)S(1)}, bf16[8,8192]{1,0:T(8,128)(2,1)S(1)}) fusion(f32[]{:T(128)S(6)} %div.51, s32[]{:T(128)S(6)} %select_n.237, s32[8192]{0:T(1024)S(1)} %multiply_add_fusion.2, s32[8]{0:T(128)S(1)} %get-tuple-element.489, pred[]{:T(512)S(6)} %lt.181), kind=kLoop, calls=%fused_computation.24.clone.1 | loop fusion | flops 786432 | bytes 294953 | tf_op jit(solution)/shard_map/convert.5
  45.7 1.0 constant_dynamic-slice_fusion.4
  51.8 3.7 %cosine_convert_fusion.2 = (bf16[8,8192]{1,0:T(8,128)(2,1)S(1)}, bf16[8,8192]{1,0:T(8,128)(2,1)S(1)}) fusion(f32[]{:T(128)S(6)} %div.51, s32[]{:T(128)S(6)} %select_n.237, s32[8192]{0:T(1024)S(1)} %multiply_add_fusion.2, s32[8]{0:T(128)S(1)} %get-tuple-element.489, pred[]{:T(512)S(6)} %lt.181), kind=kLoop, calls=%fused_computation.24.clone.1 | loop fusion | flops 786432 | bytes 294953 | tf_op jit(solution)/shard_map/convert.5
  56.2 1.0 constant_dynamic-slice_fusion.4
  62.3 3.7 %cosine_convert_fusion.2 = (bf16[8,8192]{1,0:T(8,128)(2,1)S(1)}, bf16[8,8192]{1,0:T(8,128)(2,1)S(1)}) fusion(f32[]{:T(128)S(6)} %div.51, s32[]{:T(128)S(6)} %select_n.237, s32[8192]{0:T(1024)S(1)} %multiply_add_fusion.2, s32[8]{0:T(128)S(1)} %get-tuple-element.489, pred[]{:T(512)S(6)} %lt.181), kind=kLoop, calls=%fused_computation.24.clone.1 | loop fusion | flops 786432 | bytes 294953 | tf_op jit(solution)/shard_map/convert.5
  66.8 1.0 constant_dynamic-slice_fusion.4
  72.8 3.7 %cosine_convert_fusion.2 = (bf16[8,8192]{1,0:T(8,128)(2,1)S(1)}, bf16[8,8192]{1,0:T(8,128)(2,1)S(1)}) fusion(f32[]{:T(128)S(6)} %div.51, s32[]{:T(128)S(6)} %select_n.237, s32[8192]{0:T(1024)S(1)} %multiply_add_fusion.2, s32[8]{0:T(128)S(1)} %get-tuple-element.489, pred[]{:T(512)S(6)} %lt.181), kind=kLoop, calls=%fused_computation.24.clone.1 | loop fusion | flops 786432 | bytes 294953 | tf_op jit(solution)/shard_map/convert.5
  77.3 1.0 constant_dynamic-slice_fusion.4
  79.6 4.5 %all-to-all-start.1 = ((bf16[1,4,8,4]{1,3,0,2:T(4,128)(2,1)}), bf16[1,4,8,4]{1,3,0,2:T(4,128)(2,1)S(1)}, u32[]{:S(2)}, u32[]{:S(2)}) async-start(bf16[1,4,8,4]{1,3,0,2:T(4,128)(2,1)} %copy.43), calls=%async_computation.1 | async-start | bytes 16384 | tf_op jit(solution)/shard_map/all_to_all | solution.py:158
  84.1 4.2 %all-to-all-done.1 = bf16[1,4,8,4]{1,3,0,2:T(4,128)(2,1)S(1)} async-done(((bf16[1,4,8,4]{1,3,0,2:T(4,128)(2,1)}), bf16[1,4,8,4]{1,3,0,2:T(4,128)(2,1)S(1)}, u32[]{:S(2)}, u32[]{:S(2)}) %all-to-all-start.1) | async-done | bytes 288 | tf_op jit(solution)/shard_map/all_to_all | solution.py:158
  89.0 8.8 %while.39 = (s32[]{:T(128)}, f32[4,4096]{1,0:T(4,128)S(1)}, bf16[2,1,4096,32]{2,3,1,0:T(8,128)(2,1)}, bf16[4,32]{1,0:T(4,128)(2,1)S(1)}, bf16[4,32]{1,0:T(4,128)...) while((s32[]{:T(128)}, f32[4,4096]{1,0:T(4,128)S(1)}, ...), condition=%wide.region_6.8_spmd, body=%wide.region_5.7_spmd.sunk | while | flops 264199 | bytes 93091 | solution.py:182
  91.7 0.9 fusion.78
  93.4 0.9 fusion.78
  97.9 2.8 %collective-permute-start = (f32[1,4,1,1024]{3,1,2,0:T(4,128)S(1)}, f32[1,4,1,1024]{3,1,2,0:T(4,128)S(1)}, u32[]{:S(2)}, u32[]{:S(2)}) collective-permute-start(f32[1,4,1,1024]{3,1,2,0:T(4,128)S(1)} %get-tuple-element.293), channel_id=1, source_target_pairs={{0,8},{8,0},{16,24},{24,16},{1,9},{9,1},{17,25},{25,17},{2,10},{10... | collective-permute-start | bytes 49160 | tf_op jit(solution)/shard_map/ppermute | solution.py:25
  100.7 1.2 %collective-permute-start.1 = (f32[1,4,1,1024]{3,1,2,0:T(4,128)S(1)}, f32[1,4,1,1024]{3,1,2,0:T(4,128)S(1)}, u32[]{:S(2)}, u32[]{:S(2)}) collective-permute-start(f32[1,4,1,1024]{3,1,2,0:T(4,128)S(1)} %get-tuple-element.292), channel_id=1, source_target_pairs={{0,16},{8,24},{16,0},{24,8},{1,17},{9,25},{17,1},{25,9},{2,18},{10... | collective-permute-start | bytes 49160 | tf_op jit(solution)/shard_map/ppermute | solution.py:25
  103.3 1.8 %collective-permute-done.2 = f32[1,4,1,1024]{3,1,2,0:T(4,128)S(1)} collective-permute-done((f32[1,4,1,1024]{3,1,2,0:T(4,128)S(1)}, f32[1,4,1,1024]{3,1,2,0:T(4,128)S(1)}, u32[]{:S(2)}, u32[]{:S(2)}) %collective-permute-start.2) | collective-permute-done | bytes 16416 | tf_op jit(solution)/shard_map/ppermute | solution.py:25
  (129 shorter events, 29.6 us)
Async XLA Ops:
  0.0 0.7 copy-start.2
  0.0 3.8 %copy-start.4 = (s32[32]{0:T(128)S(1)}, s32[32]{0:T(128)}, u32[]{:S(2)}) copy-start(s32[32]{0:T(128)} %param.24) | copy-start | bytes 388
  0.0 3.9 %copy-start.3 = (s32[4]{0:T(128)S(1)}, s32[4]{0:T(128)}, u32[]{:S(2)}) copy-start(s32[4]{0:T(128)} %param.22) | copy-start | bytes 52
  0.7 7.3 %copy-start.1 = (f32[3,4,1,1024]{3,2,1,0:T(1,128)S(1)}, f32[3,4,1,1024]{3,2,1,0:T(1,128)}, u32[]{:S(2)}) copy-start(f32[3,4,1,1024]{3,2,1,0:T(1,128)} %param.17) | copy-start | bytes 147460
  6.4 0.9 copy-start
  27.2 8.9 %all-to-all-start = ((bf16[1,4,1,32]{1,2,0,3:T(2,128)(2,1)}), bf16[1,4,1,32]{1,2,0,3:T(2,128)(2,1)S(1)}, u32[]{:S(2)}, u32[]{:S(2)}) async-start(bf16[1,4,1,32]{1,2,0,3:T(2,128)(2,1)} %copy.39), calls=%async_computation | async-start | bytes 32768 | tf_op jit(solution)/shard_map/all_to_all | solution.py:147
  36.1 0.7 copy-start.5
  79.6 8.7 %all-to-all-start.1 = ((bf16[1,4,8,4]{1,3,0,2:T(4,128)(2,1)}), bf16[1,4,8,4]{1,3,0,2:T(4,128)(2,1)S(1)}, u32[]{:S(2)}, u32[]{:S(2)}) async-start(bf16[1,4,8,4]{1,3,0,2:T(4,128)(2,1)} %copy.43), calls=%async_computation.1 | async-start | bytes 16384 | tf_op jit(solution)/shard_map/all_to_all | solution.py:158
  97.9 5.1 %collective-permute-start = (f32[1,4,1,1024]{3,1,2,0:T(4,128)S(1)}, f32[1,4,1,1024]{3,1,2,0:T(4,128)S(1)}, u32[]{:S(2)}, u32[]{:S(2)}) collective-permute-start(f32[1,4,1,1024]{3,1,2,0:T(4,128)S(1)} %get-tuple-element.293), channel_id=1, source_target_pairs={{0,8},{8,0},{16,24},{24,16},{1,9},{9,1},{17,25},{25,17},{2,10},{10... | collective-permute-start | bytes 49160 | tf_op jit(solution)/shard_map/ppermute | solution.py:25
  100.7 2.6 %collective-permute-start.1 = (f32[1,4,1,1024]{3,1,2,0:T(4,128)S(1)}, f32[1,4,1,1024]{3,1,2,0:T(4,128)S(1)}, u32[]{:S(2)}, u32[]{:S(2)}) collective-permute-start(f32[1,4,1,1024]{3,1,2,0:T(4,128)S(1)} %get-tuple-element.292), channel_id=1, source_target_pairs={{0,16},{8,24},{16,0},{24,8},{1,17},{9,25},{17,1},{25,9},{2,18},{10... | collective-permute-start | bytes 49160 | tf_op jit(solution)/shard_map/ppermute | solution.py:25
  101.9 3.2 %collective-permute-start.2 = (f32[1,4,1,1024]{3,1,2,0:T(4,128)S(1)}, f32[1,4,1,1024]{3,1,2,0:T(4,128)S(1)}, u32[]{:S(2)}, u32[]{:S(2)}) collective-permute-start(f32[1,4,1,1024]{3,1,2,0:T(4,128)S(1)} %get-tuple-element.291), channel_id=1, source_target_pairs={{0,24},{8,16},{16,8},{24,0},{1,25},{9,17},{17,9},{25,1},{2,26},{10... | collective-permute-start | bytes 49160 | tf_op jit(solution)/shard_map/ppermute | solution.py:25
